TPU v7x, 512 devices: a whole 4x4x16 slice. The times are simulated.
512 devices in a mesh: group: 32 (over x, y, core), tp: 16 (over z).
Axes of the slice: x: 4, y: 4, z: 16, core: 2. Of those that a mesh axis runs over, the one named last changes fastest.
Arguments:
- tokens: bfloat16 [24576, 8192], P('group', 'tp'), may hold values from -6 to 6
- w_query: bfloat16 [8192, 4096], P(None, 'tp'), may hold values from -0.0625 to 0.0625
- adapter_down: bfloat16 [384, 16, 8192], P('group', None, 'tp'), may hold values from -0.0625 to 0.0625
- adapter_up: bfloat16 [384, 16, 4096], P('group', None, 'tp'), may hold values from -1.5 to 1.5
- adapter_id: int32 [24576], P('group'), may hold values from 0 to 383, as said below
Outputs:
- query: bfloat16 [24576, 4096], P('group', 'tp')
Inputs may be any that keep to these rules, and one draw needn't show every extreme that they name: `adapter_id`: adapter a is owned by group a // 12. Among the 768 requests of one group (an aligned block), at most 48 use adapters of any one owner; in every draw one owner receives exactly 48 from every group.
All inputs are finite; a program needn't handle non-finite values.
Results may differ from a plain program's by a relative error of at most 0.014.
Values may be sent and summed in bfloat16 or wider, within the bound.
No kernel may reach another device: no remote copies, remote signals or barrier semaphores. Data moves between devices by JAX's collectives and lax.ppermute only.
A program may use at most 128 MiB of HBM per device.

v0:
```python
import jax
import jax.numpy as jnp
from jax import lax
from jax.sharding import PartitionSpec as P

adapter_scale_factor = 2.0


def on_device(tokens, w_query, adapter_down, adapter_up, adapter_id):
    pool_down, pool_up = (
        lax.all_gather(adapter_down, "group", axis=0, tiled=True),
        lax.all_gather(adapter_up, "group", axis=0, tiled=True),
    )
    picked_down = jnp.take(pool_down, adapter_id, axis=0)
    partial_value = jnp.einsum(
        "nd,nrd->nr", tokens, picked_down, preferred_element_type=jnp.float32
    )
    total_output = lax.psum(partial_value, "tp")
    scaled_delta = (adapter_scale_factor * total_output).astype(jnp.bfloat16)
    picked_up = jnp.take(pool_up, adapter_id, axis=0)
    delta_rows = jnp.einsum(
        "nr,nrh->nh", scaled_delta, picked_up, preferred_element_type=jnp.float32
    ).astype(jnp.bfloat16)
    base = jnp.dot(
        lax.all_gather(tokens, "tp", axis=1, tiled=True),
        w_query,
        preferred_element_type=jnp.float32,
    )
    return (base + delta_rows.astype(jnp.float32)).astype(jnp.bfloat16)


def solution(mesh):
    placed = (
        P("group", "tp"),
        P(None, "tp"),
        P("group", None, "tp"),
        P("group", None, "tp"),
        P("group"),
    )
    return jax.shard_map(
        on_device, mesh=mesh, in_specs=placed, out_specs=P("group", "tp"), check_vma=False
    )
```

profile of v0, /device:TPU:1, one launch (start us, length us, event | category | flops | bytes accessed | tf_op | source)
XLA Modules:
  0.0 317.1 jit_solution(11295828361454792933)
XLA Ops:
  6.5 0.0 all-gather.8.cloned.1.call-start
  6.5 0.7 all-gather.8.cloned.1.call-update
  7.3 0.0 all-gather.6.cloned.1.call-start
  7.3 0.7 all-gather.6.cloned.1.call-update
  8.0 0.0 all-gather.4.cloned.1.call-start
  8.1 0.7 all-gather.4.cloned.1.call-update
  8.7 0.7 compare_select_fusion
  9.4 0.7 compare_and_fusion
  10.1 66.6 %all-gather.8.cloned.1.call-done = bf16[384,16,256]{2,1,0:T(8,128)(2,1)} async-done(((bf16[12,16,256]{2,1,0:T(8,128)(2,1)}), bf16[384,16,256]{2,1,0:T(8,128)(2,1)}) %all-gather.8.cloned.1.call-update) | async-done | bytes 3145744 | tf_op jit(solution)/shard_map/all_gather | solution.py:12
  76.7 7.0 %gather_fusion.1 = bf16[768,16,256]{2,1,0:T(8,128)(2,1)} fusion(bf16[384,16,256]{2,1,0:T(8,128)(2,1)} %all-gather.8.cloned.1.call-done, s32[1024]{0:T(1024)S(1)} %pad_clamp_fusion), kind=kCustom, calls=%fused_computation.1 | custom fusion | bytes 12585984 | tf_op jit(solution)/shard_map/jit(_take)/gather | solution.py:20
  83.6 0.0 copy-start
  83.6 60.0 %all-gather.6.cloned.1.call-done = bf16[384,16,512]{2,1,0:T(8,128)(2,1)} async-done(((bf16[12,16,512]{2,1,0:T(8,128)(2,1)}), bf16[384,16,512]{2,1,0:T(8,128)(2,1)}) %all-gather.6.cloned.1.call-update) | async-done | bytes 6291472 | tf_op jit(solution)/shard_map/all_gather | solution.py:11
  143.7 22.4 %gather_fusion = bf16[768,16,512]{2,1,0:T(8,128)(2,1)} fusion(bf16[384,16,512]{2,1,0:T(8,128)(2,1)} %all-gather.6.cloned.1.call-done, s32[1024]{0:T(1024)S(1)} %pad_clamp_fusion), kind=kCustom, calls=%fused_computation | custom fusion | bytes 25168896 | tf_op jit(solution)/shard_map/jit(_take)/gather | solution.py:14
  166.1 0.0 copy-done
  166.1 9.9 %fusion = f32[768,1,16]{2,1,0:T(1,128)S(1)} fusion(bf16[768,16,512]{2,1,0:T(8,128)(2,1)} %gather_fusion, pred[768]{0:T(1024)(128)(4,1)S(1)} %compare_and_fusion, bf16[768,512,1]{1,0,2:T(8,128)(2,1)S(1)} %bitcast.11), kind=kOutput, calls=%fused_computation.2 | convolution fusion | flops 18874368 | bytes 13419264 | tf_op jit(solution)/shard_map/nd,nrd->nr/dot_general | solution.py:15
  176.1 61.4 %psum.7 = f32[768,16]{1,0:T(8,128)S(1)} all-reduce(f32[768,16]{1,0:T(8,128)S(1)} %bitcast.12), channel_id=1, replica_groups=mesh['group'=32,'tp'=16] {'tp'}, use_global_device_ids=true, to_apply=%region_0.1 | all-reduce | flops 12288 | bytes 98304 | tf_op jit(solution)/shard_map/psum | solution.py:18
  237.5 8.5 %fusion.3 = bf16[768,1,256]{2,1,0:T(2,128)(2,1)S(1)} fusion(bf16[768,16,256]{2,1,0:T(8,128)(2,1)} %gather_fusion.1, pred[768]{0:T(1024)(128)(4,1)S(1)} %compare_and_fusion, bf16[768,16,1]{1,0,2:T(8,128)(2,1)S(1)} %fusion.11), kind=kOutput, calls=%fused_computation.5 | convolution fusion | flops 9437184 | bytes 6710016 | tf_op jit(solution)/shard_map/nr,nrh->nh/dot_general | solution.py:21
  246.0 54.7 %all-gather.4.cloned.1.call-done = bf16[768,8192]{1,0:T(8,128)(2,1)} async-done(((bf16[768,512]{1,0:T(8,128)(2,1)}), bf16[768,8192]{1,0:T(8,128)(2,1)}) %all-gather.4.cloned.1.call-update) | async-done | bytes 12582928 | tf_op jit(solution)/shard_map/all_gather | solution.py:25
  300.7 9.9 %fusion.9 = bf16[768,256]{1,0:T(8,128)(2,1)} fusion(bf16[768,8192]{1,0:T(8,128)(2,1)} %all-gather.4.cloned.1.call-done, bf16[8192,256]{1,0:T(8,128)(2,1)} %param.6, bf16[768,1,256]{2,1,0:T(2,128)(2,1)S(1)} %fusion.3), kind=kOutput, calls=%fused_computation.12 | convolution fusion | flops 3221815296 | bytes 17563648 | tf_op jit(solution)/shard_map/dot_general | solution.py:24
  (2 shorter events, 0.0 us)
Async XLA Ops:
  6.5 70.2 %all-gather.8.cloned.1.call-start = ((), (), s32[]{:S(2)}) async-start(), calls=%async_computation.2 | async-start | bytes 3244032 | tf_op jit(solution)/shard_map/all_gather | solution.py:12
  7.3 136.4 %all-gather.6.cloned.1.call-start = ((), (), s32[]{:S(2)}) async-start(), calls=%async_computation.1 | async-start | bytes 6488064 | tf_op jit(solution)/shard_map/all_gather | solution.py:11
  8.0 292.7 %all-gather.4.cloned.1.call-start = ((), (), s32[]{:S(2)}) async-start(), calls=%async_computation | async-start | bytes 13369344 | tf_op jit(solution)/shard_map/all_gather | solution.py:25
  83.6 82.5 %copy-start = (bf16[768,512]{1,0:T(8,128)(2,1)S(1)}, bf16[768,512]{1,0:T(8,128)(2,1)}, u32[]{:S(2)}) copy-start(bf16[768,512]{1,0:T(8,128)(2,1)} %param.5) | copy-start | bytes 2359300
Sparse Core Ops, SparseCore 0:
  10.5 66.1 all-gather.7
  79.8 63.8 all-gather.5
  145.8 154.8 all-gather.3
where the time goes:
time: 317 us
  waiting for transfers between devices  183 us (58%)
  blocking collectives  61.4 us (19%)
  local copies, waits for them, and re-layouts  29.4 us (9%)
  matrix products  28.3 us (9%)
  between operations  13.2 us (4%)
    all_gather x1, waiting for transfers between devices, on_device(): lax.all_gather(adapter_up, 'group', axis=0, tiled=True)  66.6 us
    psum x1, blocking collectives, on_device(): total_output = lax.psum(partial_value, 'tp')  61.4 us
    all_gather x1, waiting for transfers between devices, on_device(): lax.all_gather(adapter_down, 'group', axis=0, tiled=True)  60 us
    all_gather x1, waiting for transfers between devices, on_device(): lax.all_gather(tokens, 'tp', axis=1, tiled=True)  54.7 us
    gather x1, local copies, waits for them, and re-layouts, on_device(): picked_down = jnp.take(pool_down, adapter_id, axis=0)  22.4 us
    dot_general x1, matrix products, on_device(): jnp.dot(lax.all_gather(tokens, 'tp', axis=1, tiled=True), w_query, prefer...  9.92 us
    dot_general x1, matrix products, on_device(): jnp.einsum('nd,nrd->nr', tokens, picked_down, preferred_element_type=jnp....  9.91 us
    dot_general x1, matrix products, on_device(): jnp.einsum('nr,nrh->nh', scaled_delta, picked_up, preferred_element_type=...  8.51 us
  transfers between devices with their start and end apart: 3, of which 3 were waited for; matrix products, arithmetic and copies ran while one was open for 16% of the time, Pallas kernels for 0%

commit v1 on v0

--- a/solution.py
+++ b/solution.py
@@ -4,6 +4,37 @@
 from jax.sharding import PartitionSpec as P
 
 adapter_scale_factor = 2.0
+
+
+def routes_all_review(own_rows, dim_i):
+    passed = lax.axis_index("tp")
+    base_arr = lax.axis_size("tp")
+    state_next, upper, local_next = (base_arr, passed, own_rows.shape[dim_i])
+    steps_seen = list(map(lambda it: (it, (it + 1) % state_next), range(state_next)))
+    later = map(lambda it: (it, (it - 1) % state_next), range(state_next))
+    current_block = jnp.zeros(
+        (*own_rows.shape[:dim_i], state_next * local_next, *own_rows.shape[dim_i + 1 :]),
+        own_rows.dtype,
+    )
+    current_block = lax.dynamic_update_slice_in_dim(
+        current_block, own_rows, upper * local_next, axis=dim_i
+    )
+    grid = list(later)
+    big = state_next // 2
+    z_new = d_next = own_rows
+    w = 1
+    while w < big + 1:
+        z_new = lax.ppermute(z_new, axis_name="tp", perm=steps_seen)
+        current_block = lax.dynamic_update_slice_in_dim(
+            current_block, z_new, (upper - w) % state_next * local_next, axis=dim_i
+        )
+        if w < state_next - big:
+            d_next = lax.ppermute(d_next, axis_name="tp", perm=grid)
+            current_block = lax.dynamic_update_slice_in_dim(
+                current_block, d_next, (upper + w) % state_next * local_next, axis=dim_i
+            )
+        w = w + 1
+    return current_block
 
 
 def on_device(tokens, w_query, adapter_down, adapter_up, adapter_id):
@@ -21,11 +52,7 @@
     delta_rows = jnp.einsum(
         "nr,nrh->nh", scaled_delta, picked_up, preferred_element_type=jnp.float32
     ).astype(jnp.bfloat16)
-    base = jnp.dot(
-        lax.all_gather(tokens, "tp", axis=1, tiled=True),
-        w_query,
-        preferred_element_type=jnp.float32,
-    )
+    base = jnp.dot(routes_all_review(tokens, 1), w_query, preferred_element_type=jnp.float32)
     return (base + delta_rows.astype(jnp.float32)).astype(jnp.bfloat16)
 
 

time: 317 us -> 291 us (0.918)
  the two profiles are of different devices: /device:TPU:1 before, /device:TPU:24 now
where the time goes in v1:
time: 291 us; the launch traced here: 290 us
  waiting for transfers between devices  75.6 us (26%)
  blocking collectives  60 us (21%)
  starting transfers between devices  58.1 us (20%)
  local copies, waits for them, and re-layouts  55.8 us (19%)
  matrix products  25.9 us (9%)
  between operations  13.7 us (5%)
    ppermute x8, waiting for transfers between devices, routes_all_review(): z_new = lax.ppermute(z_new, axis_name='tp', perm=steps_seen)  70.9 us
    psum x1, blocking collectives, on_device(): total_output = lax.psum(partial_value, 'tp')  60 us
    ppermute x7, starting transfers between devices, routes_all_review(): d_next = lax.ppermute(d_next, axis_name='tp', perm=grid)  40.7 us
    gather x1, local copies, waits for them, and re-layouts, on_device(): picked_down = jnp.take(pool_down, adapter_id, axis=0)  22.4 us
    ppermute x8, starting transfers between devices, routes_all_review(): z_new = lax.ppermute(z_new, axis_name='tp', perm=steps_seen)  17.4 us
    dynamic_update_slice x8, local copies, waits for them, and re-layouts, routes_all_review(): lax.dynamic_update_slice_in_dim(current_block, z_new, (upper - w) % state...  10.1 us
    dot_general x1, matrix products, on_device(): jnp.einsum('nd,nrd->nr', tokens, picked_down, preferred_element_type=jnp....  9.89 us
    dynamic_update_slice x7, local copies, waits for them, and re-layouts, routes_all_review(): lax.dynamic_update_slice_in_dim(current_block, d_next, (upper + w) % stat...  9.18 us
  transfers between devices with their start and end apart: 17, of which 8 were waited for; matrix products, arithmetic and copies ran while one was open for 12% of the time, Pallas kernels for 0%

profile of v1, /device:TPU:24, one launch (start us, length us, event | category | flops | bytes accessed | tf_op | source)
XLA Modules:
  0.0 289.9 jit_solution(10413746270445385759)
XLA Ops:
  8.0 3.8 %collective-permute-start = (bf16[768,512]{1,0:T(8,128)(2,1)}, bf16[768,512]{1,0:T(8,128)(2,1)S(1)}, u32[]{:S(2)}, u32[]{:S(2)}) collective-permute-start(bf16[768,512]{1,0:T(8,128)(2,1)} %param.5), channel_id=1, source_target_pairs={{0,1},{1,2},{2,3},{3,4},{4,5},{5,6},{6,7},{7,8},{8,9},{9,10},{10,1... | collective-permute-start | bytes 2359304 | tf_op jit(solution)/shard_map/ppermute | solution.py:27
  11.8 9.5 %collective-permute-start.1 = (bf16[768,512]{1,0:T(8,128)(2,1)}, bf16[768,512]{1,0:T(8,128)(2,1)S(1)}, u32[]{:S(2)}, u32[]{:S(2)}) collective-permute-start(bf16[768,512]{1,0:T(8,128)(2,1)} %param.5), channel_id=1, source_target_pairs={{0,15},{1,0},{2,1},{3,2},{4,3},{5,4},{6,5},{7,6},{8,7},{9,8},{10,9... | collective-permute-start | bytes 2359304 | tf_op jit(solution)/shard_map/ppermute | solution.py:32
  21.3 15.8 %collective-permute-done = bf16[768,512]{1,0:T(8,128)(2,1)S(1)} collective-permute-done((bf16[768,512]{1,0:T(8,128)(2,1)}, bf16[768,512]{1,0:T(8,128)(2,1)S(1)}, u32[]{:S(2)}, u32[]{:S(2)}) %collective-permute-start) | collective-permute-done | bytes 786464 | tf_op jit(solution)/shard_map/ppermute | solution.py:27
  37.2 1.9 collective-permute-start.2
  39.1 5.1 %collective-permute-start.3 = (bf16[768,512]{1,0:T(8,128)(2,1)S(1)}, bf16[768,512]{1,0:T(8,128)(2,1)S(1)}, u32[]{:S(2)}, u32[]{:S(2)}) collective-permute-start(bf16[768,512]{1,0:T(8,128)(2,1)S(1)} %collective-permute-done.1), channel_id=1, source_target_pairs={{0,15},{1,0},{2,1},{3,2},{4,3},{5,4},{6,5},{7,6},{8,7},{9,8},{10,9... | collective-permute-start | bytes 2359304 | tf_op jit(solution)/shard_map/ppermute | solution.py:32
  44.2 14.7 %collective-permute-done.2 = bf16[768,512]{1,0:T(8,128)(2,1)S(1)} collective-permute-done((bf16[768,512]{1,0:T(8,128)(2,1)S(1)}, bf16[768,512]{1,0:T(8,128)(2,1)S(1)}, u32[]{:S(2)}, u32[]{:S(2)}) %collective-permute-start.2) | collective-permute-done | bytes 786464 | tf_op jit(solution)/shard_map/ppermute | solution.py:27
  59.0 1.9 collective-permute-start.4
  60.9 5.1 %collective-permute-start.5 = (bf16[768,512]{1,0:T(8,128)(2,1)S(1)}, bf16[768,512]{1,0:T(8,128)(2,1)S(1)}, u32[]{:S(2)}, u32[]{:S(2)}) collective-permute-start(bf16[768,512]{1,0:T(8,128)(2,1)S(1)} %collective-permute-done.3), channel_id=1, source_target_pairs={{0,15},{1,0},{2,1},{3,2},{4,3},{5,4},{6,5},{7,6},{8,7},{9,8},{10,9... | collective-permute-start | bytes 2359304 | tf_op jit(solution)/shard_map/ppermute | solution.py:32
  66.0 13.8 %collective-permute-done.4 = bf16[768,512]{1,0:T(8,128)(2,1)S(1)} collective-permute-done((bf16[768,512]{1,0:T(8,128)(2,1)S(1)}, bf16[768,512]{1,0:T(8,128)(2,1)S(1)}, u32[]{:S(2)}, u32[]{:S(2)}) %collective-permute-start.4) | collective-permute-done | bytes 786464 | tf_op jit(solution)/shard_map/ppermute | solution.py:27
  79.9 1.9 collective-permute-start.6
  81.8 5.1 %collective-permute-start.7 = (bf16[768,512]{1,0:T(8,128)(2,1)S(1)}, bf16[768,512]{1,0:T(8,128)(2,1)}, u32[]{:S(2)}, u32[]{:S(2)}) collective-permute-start(bf16[768,512]{1,0:T(8,128)(2,1)S(1)} %collective-permute-done.5), channel_id=1, source_target_pairs={{0,15},{1,0},{2,1},{3,2},{4,3},{5,4},{6,5},{7,6},{8,7},{9,8},{10,9... | collective-permute-start | bytes 2359304 | tf_op jit(solution)/shard_map/ppermute | solution.py:32
  87.0 12.9 %collective-permute-done.6 = bf16[768,512]{1,0:T(8,128)(2,1)S(1)} collective-permute-done((bf16[768,512]{1,0:T(8,128)(2,1)S(1)}, bf16[768,512]{1,0:T(8,128)(2,1)S(1)}, u32[]{:S(2)}, u32[]{:S(2)}) %collective-permute-start.6) | collective-permute-done | bytes 786464 | tf_op jit(solution)/shard_map/ppermute | solution.py:27
  99.9 1.9 collective-permute-start.8
  101.8 5.1 %collective-permute-start.9 = (bf16[768,512]{1,0:T(8,128)(2,1)}, bf16[768,512]{1,0:T(8,128)(2,1)}, u32[]{:S(2)}, u32[]{:S(2)}) collective-permute-start(bf16[768,512]{1,0:T(8,128)(2,1)} %collective-permute-done.7), channel_id=1, source_target_pairs={{0,15},{1,0},{2,1},{3,2},{4,3},{5,4},{6,5},{7,6},{8,7},{9,8},{10,9... | collective-permute-start | bytes 2359304 | tf_op jit(solution)/shard_map/ppermute | solution.py:32
  106.9 12.1 %collective-permute-done.8 = bf16[768,512]{1,0:T(8,128)(2,1)} collective-permute-done((bf16[768,512]{1,0:T(8,128)(2,1)S(1)}, bf16[768,512]{1,0:T(8,128)(2,1)}, u32[]{:S(2)}, u32[]{:S(2)}) %collective-permute-start.8) | collective-permute-done | bytes 786464 | tf_op jit(solution)/shard_map/ppermute | solution.py:27
  119.0 1.9 collective-permute-start.10
  121.7 6.1 %broadcast_in_dim.25 = bf16[768,8192]{1,0:T(8,128)(2,1)} broadcast(bf16[]{:T(256)} %constant.114.clone.1), dimensions={} | broadcast | bytes 12582914 | tf_op jit(solution)/shard_map/broadcast_in_dim | solution.py:15
  129.7 5.3 %collective-permute-start.11 = (bf16[768,512]{1,0:T(8,128)(2,1)}, bf16[768,512]{1,0:T(8,128)(2,1)S(1)}, u32[]{:S(2)}, u32[]{:S(2)}) collective-permute-start(bf16[768,512]{1,0:T(8,128)(2,1)} %collective-permute-done.9), channel_id=1, source_target_pairs={{0,15},{1,0},{2,1},{3,2},{4,3},{5,4},{6,5},{7,6},{8,7},{9,8},{10,9... | collective-permute-start | bytes 2359304 | tf_op jit(solution)/shard_map/ppermute | solution.py:32
  137.5 1.9 collective-permute-start.12
  144.3 3.3 %collective-permute-done.11 = bf16[768,512]{1,0:T(8,128)(2,1)S(1)} collective-permute-done((bf16[768,512]{1,0:T(8,128)(2,1)}, bf16[768,512]{1,0:T(8,128)(2,1)S(1)}, u32[]{:S(2)}, u32[]{:S(2)}) %collective-permute-start.11) | collective-permute-done | bytes 786464 | tf_op jit(solution)/shard_map/ppermute | solution.py:32
  147.6 5.4 %collective-permute-start.13 = (bf16[768,512]{1,0:T(8,128)(2,1)S(1)}, bf16[768,512]{1,0:T(8,128)(2,1)S(1)}, u32[]{:S(2)}, u32[]{:S(2)}) collective-permute-start(bf16[768,512]{1,0:T(8,128)(2,1)S(1)} %collective-permute-done.11), channel_id=1, source_target_pairs={{0,15},{1,0},{2,1},{3,2},{4,3},{5,4},{6,5},{7,6},{8,7},{9,8},{10,9... | collective-permute-start | bytes 2359304 | tf_op jit(solution)/shard_map/ppermute | solution.py:32
  152.9 2.1 constant_dynamic-update-slice_fusion.7
  155.2 2.1 collective-permute-start.14
  157.3 2.1 constant_dynamic-update-slice_fusion.6
  159.4 2.1 constant_dynamic-update-slice_fusion.5
  161.5 2.2 constant_dynamic-update-slice_fusion.4
  166.7 7.0 %gather_fusion.1 = bf16[768,16,256]{2,1,0:T(8,128)(2,1)} fusion(bf16[384,16,256]{2,1,0:T(8,128)(2,1)} %all-gather.5.cloned.1.call-done, s32[1024]{0:T(1024)S(1)} %pad_clamp_fusion), kind=kCustom, calls=%fused_computation.1 | custom fusion | bytes 12585984 | tf_op jit(solution)/shard_map/jit(_take)/gather | solution.py:51
  174.6 22.4 %gather_fusion = bf16[768,16,512]{2,1,0:T(8,128)(2,1)} fusion(bf16[384,16,512]{2,1,0:T(8,128)(2,1)} %all-gather.3.cloned.1.call-done, s32[1024]{0:T(1024)S(1)} %pad_clamp_fusion), kind=kCustom, calls=%fused_computation | custom fusion | bytes 25168896 | tf_op jit(solution)/shard_map/jit(_take)/gather | solution.py:45
  197.1 9.9 %fusion = f32[768,1,16]{2,1,0:T(1,128)S(1)} fusion(bf16[768,16,512]{2,1,0:T(8,128)(2,1)} %gather_fusion, pred[768]{0:T(1024)(128)(4,1)S(1)} %compare_and_fusion, bf16[768,512,1]{1,0,2:T(8,128)(2,1)S(1)} %bitcast.11), kind=kOutput, calls=%fused_computation.2 | convolution fusion | flops 18874368 | bytes 13419264 | tf_op jit(solution)/shard_map/nd,nrd->nr/dot_general | solution.py:46
  207.0 60.0 %psum.7 = f32[768,16]{1,0:T(8,128)S(1)} all-reduce(f32[768,16]{1,0:T(8,128)S(1)} %bitcast.12), channel_id=1, replica_groups=mesh['group'=32,'tp'=16] {'tp'}, use_global_device_ids=true, to_apply=%region_0.1 | all-reduce | flops 12288 | bytes 98304 | tf_op jit(solution)/shard_map/psum | solution.py:49
  267.0 8.7 %fusion.3 = bf16[768,1,256]{2,1,0:T(2,128)(2,1)S(1)} fusion(bf16[768,16,256]{2,1,0:T(8,128)(2,1)} %gather_fusion.1, pred[768]{0:T(1024)(128)(4,1)S(1)} %compare_and_fusion, bf16[768,16,1]{1,0,2:T(8,128)(2,1)S(1)} %fusion.11), kind=kOutput, calls=%fused_computation.5 | convolution fusion | flops 9437184 | bytes 6710016 | tf_op jit(solution)/shard_map/nr,nrh->nh/dot_general | solution.py:52
  275.7 7.3 %fusion.9 = bf16[768,256]{1,0:T(8,128)(2,1)} fusion(bf16[768,8192]{1,0:T(8,128)(2,1)} %constant_dynamic-update-slice_fusion, bf16[8192,256]{1,0:T(8,128)(2,1)S(1)} %copy-done.10, bf16[768,1,256]{2,1,0:T(2,128)(2,1)S(1)} %fusion.3), kind=kOutput, calls=%fused_computation.12 | convolution fusion | flops 3221815296 | bytes 17563648 | tf_op jit(solution)/shard_map/dot_general | solution.py:55
  (53 shorter events, 15.6 us)
Async XLA Ops:
  6.5 121.2 %copy-start = (bf16[768,512]{1,0:T(8,128)(2,1)S(1)}, bf16[768,512]{1,0:T(8,128)(2,1)}, u32[]{:S(2)}) copy-start(bf16[768,512]{1,0:T(8,128)(2,1)} %param.5) | copy-start | bytes 2359300
  6.5 122.2 %copy-start.9 = (s32[768]{0:T(1024)S(1)}, s32[768]{0:T(1024)}, u32[]{:S(2)}) copy-start(s32[768]{0:T(1024)} %param.9) | copy-start | bytes 9220
  6.5 160.1 %all-gather.5.cloned.1.call-start = ((), (), s32[]{:S(2)}) async-start(), calls=%async_computation.1 | async-start | bytes 3244032 | tf_op jit(solution)/shard_map/all_gather | solution.py:43
  7.3 167.4 %all-gather.3.cloned.1.call-start = ((), (), s32[]{:S(2)}) async-start(), calls=%async_computation | async-start | bytes 6488064 | tf_op jit(solution)/shard_map/all_gather | solution.py:42
  8.0 29.1 %collective-permute-start = (bf16[768,512]{1,0:T(8,128)(2,1)}, bf16[768,512]{1,0:T(8,128)(2,1)S(1)}, u32[]{:S(2)}, u32[]{:S(2)}) collective-permute-start(bf16[768,512]{1,0:T(8,128)(2,1)} %param.5), channel_id=1, source_target_pairs={{0,1},{1,2},{2,3},{3,4},{4,5},{5,6},{6,7},{7,8},{8,9},{9,10},{10,1... | collective-permute-start | bytes 2359304 | tf_op jit(solution)/shard_map/ppermute | solution.py:27
  11.8 27.2 %collective-permute-start.1 = (bf16[768,512]{1,0:T(8,128)(2,1)}, bf16[768,512]{1,0:T(8,128)(2,1)S(1)}, u32[]{:S(2)}, u32[]{:S(2)}) collective-permute-start(bf16[768,512]{1,0:T(8,128)(2,1)} %param.5), channel_id=1, source_target_pairs={{0,15},{1,0},{2,1},{3,2},{4,3},{5,4},{6,5},{7,6},{8,7},{9,8},{10,9... | collective-permute-start | bytes 2359304 | tf_op jit(solution)/shard_map/ppermute | solution.py:32
  37.2 7.1 %copy-start.5 = (bf16[768,512]{1,0:T(8,128)(2,1)}, bf16[768,512]{1,0:T(8,128)(2,1)S(1)}, u32[]{:S(2)}) copy-start(bf16[768,512]{1,0:T(8,128)(2,1)S(1)} %collective-permute-done) | copy-start | bytes 2359300
  37.2 21.8 %collective-permute-start.2 = (bf16[768,512]{1,0:T(8,128)(2,1)S(1)}, bf16[768,512]{1,0:T(8,128)(2,1)S(1)}, u32[]{:S(2)}, u32[]{:S(2)}) collective-permute-start(bf16[768,512]{1,0:T(8,128)(2,1)S(1)} %collective-permute-done), channel_id=1, source_target_pairs={{0,1},{1,2},{2,3},{3,4},{4,5},{5,6},{6,7},{7,8},{8,9},{9,10},{10,1... | collective-permute-start | bytes 2359304 | tf_op jit(solution)/shard_map/ppermute | solution.py:27
  39.1 21.8 %collective-permute-start.3 = (bf16[768,512]{1,0:T(8,128)(2,1)S(1)}, bf16[768,512]{1,0:T(8,128)(2,1)S(1)}, u32[]{:S(2)}, u32[]{:S(2)}) collective-permute-start(bf16[768,512]{1,0:T(8,128)(2,1)S(1)} %collective-permute-done.1), channel_id=1, source_target_pairs={{0,15},{1,0},{2,1},{3,2},{4,3},{5,4},{6,5},{7,6},{8,7},{9,8},{10,9... | collective-permute-start | bytes 2359304 | tf_op jit(solution)/shard_map/ppermute | solution.py:32
  59.0 20.9 %collective-permute-start.4 = (bf16[768,512]{1,0:T(8,128)(2,1)S(1)}, bf16[768,512]{1,0:T(8,128)(2,1)S(1)}, u32[]{:S(2)}, u32[]{:S(2)}) collective-permute-start(bf16[768,512]{1,0:T(8,128)(2,1)S(1)} %collective-permute-done.2), channel_id=1, source_target_pairs={{0,1},{1,2},{2,3},{3,4},{4,5},{5,6},{6,7},{7,8},{8,9},{9,10},{10,1... | collective-permute-start | bytes 2359304 | tf_op jit(solution)/shard_map/ppermute | solution.py:27
  60.9 20.9 %collective-permute-start.5 = (bf16[768,512]{1,0:T(8,128)(2,1)S(1)}, bf16[768,512]{1,0:T(8,128)(2,1)S(1)}, u32[]{:S(2)}, u32[]{:S(2)}) collective-permute-start(bf16[768,512]{1,0:T(8,128)(2,1)S(1)} %collective-permute-done.3), channel_id=1, source_target_pairs={{0,15},{1,0},{2,1},{3,2},{4,3},{5,4},{6,5},{7,6},{8,7},{9,8},{10,9... | collective-permute-start | bytes 2359304 | tf_op jit(solution)/shard_map/ppermute | solution.py:32
  79.9 1.9 copy-start.1
  79.9 20.0 %collective-permute-start.6 = (bf16[768,512]{1,0:T(8,128)(2,1)S(1)}, bf16[768,512]{1,0:T(8,128)(2,1)S(1)}, u32[]{:S(2)}, u32[]{:S(2)}) collective-permute-start(bf16[768,512]{1,0:T(8,128)(2,1)S(1)} %collective-permute-done.4), channel_id=1, source_target_pairs={{0,1},{1,2},{2,3},{3,4},{4,5},{5,6},{6,7},{7,8},{8,9},{9,10},{10,1... | collective-permute-start | bytes 2359304 | tf_op jit(solution)/shard_map/ppermute | solution.py:27
  81.8 18.0 %copy-start.3 = (bf16[768,512]{1,0:T(8,128)(2,1)}, bf16[768,512]{1,0:T(8,128)(2,1)S(1)}, u32[]{:S(2)}) copy-start(bf16[768,512]{1,0:T(8,128)(2,1)S(1)} %collective-permute-done.5) | copy-start | bytes 2359300
  81.8 20.0 %collective-permute-start.7 = (bf16[768,512]{1,0:T(8,128)(2,1)S(1)}, bf16[768,512]{1,0:T(8,128)(2,1)}, u32[]{:S(2)}, u32[]{:S(2)}) collective-permute-start(bf16[768,512]{1,0:T(8,128)(2,1)S(1)} %collective-permute-done.5), channel_id=1, source_target_pairs={{0,15},{1,0},{2,1},{3,2},{4,3},{5,4},{6,5},{7,6},{8,7},{9,8},{10,9... | collective-permute-start | bytes 2359304 | tf_op jit(solution)/shard_map/ppermute | solution.py:32
  99.9 1.9 copy-start.7
  99.9 19.2 %collective-permute-start.8 = (bf16[768,512]{1,0:T(8,128)(2,1)S(1)}, bf16[768,512]{1,0:T(8,128)(2,1)}, u32[]{:S(2)}, u32[]{:S(2)}) collective-permute-start(bf16[768,512]{1,0:T(8,128)(2,1)S(1)} %collective-permute-done.6), channel_id=1, source_target_pairs={{0,1},{1,2},{2,3},{3,4},{4,5},{5,6},{6,7},{7,8},{8,9},{9,10},{10,1... | collective-permute-start | bytes 2359304 | tf_op jit(solution)/shard_map/ppermute | solution.py:27
  101.8 27.9 %collective-permute-start.9 = (bf16[768,512]{1,0:T(8,128)(2,1)}, bf16[768,512]{1,0:T(8,128)(2,1)}, u32[]{:S(2)}, u32[]{:S(2)}) collective-permute-start(bf16[768,512]{1,0:T(8,128)(2,1)} %collective-permute-done.7), channel_id=1, source_target_pairs={{0,15},{1,0},{2,1},{3,2},{4,3},{5,4},{6,5},{7,6},{8,7},{9,8},{10,9... | collective-permute-start | bytes 2359304 | tf_op jit(solution)/shard_map/ppermute | solution.py:32
  119.0 18.5 %collective-permute-start.10 = (bf16[768,512]{1,0:T(8,128)(2,1)}, bf16[768,512]{1,0:T(8,128)(2,1)}, u32[]{:S(2)}, u32[]{:S(2)}) collective-permute-start(bf16[768,512]{1,0:T(8,128)(2,1)} %collective-permute-done.8), channel_id=1, source_target_pairs={{0,1},{1,2},{2,3},{3,4},{4,5},{5,6},{6,7},{7,8},{8,9},{9,10},{10,1... | collective-permute-start | bytes 2359304 | tf_op jit(solution)/shard_map/ppermute | solution.py:27
  121.6 7.1 %copy-start.6 = (bf16[768,512]{1,0:T(8,128)(2,1)S(1)}, bf16[768,512]{1,0:T(8,128)(2,1)}, u32[]{:S(2)}) copy-start(bf16[768,512]{1,0:T(8,128)(2,1)} %copy-done.5) | copy-start | bytes 2359300
  121.6 19.7 %copy-start.2 = (bf16[768,512]{1,0:T(8,128)(2,1)S(1)}, bf16[768,512]{1,0:T(8,128)(2,1)}, u32[]{:S(2)}) copy-start(bf16[768,512]{1,0:T(8,128)(2,1)} %copy-done.1) | copy-start | bytes 2359300
  121.6 20.7 %copy-start.4 = (bf16[768,512]{1,0:T(8,128)(2,1)S(1)}, bf16[768,512]{1,0:T(8,128)(2,1)}, u32[]{:S(2)}) copy-start(bf16[768,512]{1,0:T(8,128)(2,1)} %copy-done.3) | copy-start | bytes 2359300
  121.6 21.7 %copy-start.8 = (bf16[768,512]{1,0:T(8,128)(2,1)S(1)}, bf16[768,512]{1,0:T(8,128)(2,1)}, u32[]{:S(2)}) copy-start(bf16[768,512]{1,0:T(8,128)(2,1)} %copy-done.7) | copy-start | bytes 2359300
  129.7 17.9 %collective-permute-start.11 = (bf16[768,512]{1,0:T(8,128)(2,1)}, bf16[768,512]{1,0:T(8,128)(2,1)S(1)}, u32[]{:S(2)}, u32[]{:S(2)}) collective-permute-start(bf16[768,512]{1,0:T(8,128)(2,1)} %collective-permute-done.9), channel_id=1, source_target_pairs={{0,15},{1,0},{2,1},{3,2},{4,3},{5,4},{6,5},{7,6},{8,7},{9,8},{10,9... | collective-permute-start | bytes 2359304 | tf_op jit(solution)/shard_map/ppermute | solution.py:32
  137.5 17.7 %collective-permute-start.12 = (bf16[768,512]{1,0:T(8,128)(2,1)}, bf16[768,512]{1,0:T(8,128)(2,1)S(1)}, u32[]{:S(2)}, u32[]{:S(2)}) collective-permute-start(bf16[768,512]{1,0:T(8,128)(2,1)} %collective-permute-done.10), channel_id=1, source_target_pairs={{0,1},{1,2},{2,3},{3,4},{4,5},{5,6},{6,7},{7,8},{8,9},{9,10},{10,1... | collective-permute-start | bytes 2359304 | tf_op jit(solution)/shard_map/ppermute | solution.py:27
  147.6 18.1 %collective-permute-start.13 = (bf16[768,512]{1,0:T(8,128)(2,1)S(1)}, bf16[768,512]{1,0:T(8,128)(2,1)S(1)}, u32[]{:S(2)}, u32[]{:S(2)}) collective-permute-start(bf16[768,512]{1,0:T(8,128)(2,1)S(1)} %collective-permute-done.11), channel_id=1, source_target_pairs={{0,15},{1,0},{2,1},{3,2},{4,3},{5,4},{6,5},{7,6},{8,7},{9,8},{10,9... | collective-permute-start | bytes 2359304 | tf_op jit(solution)/shard_map/ppermute | solution.py:32
  155.2 18.5 %collective-permute-start.14 = (bf16[768,512]{1,0:T(8,128)(2,1)S(1)}, bf16[768,512]{1,0:T(8,128)(2,1)S(1)}, u32[]{:S(2)}, u32[]{:S(2)}) collective-permute-start(bf16[768,512]{1,0:T(8,128)(2,1)S(1)} %collective-permute-done.12), channel_id=1, source_target_pairs={{0,1},{1,2},{2,3},{3,4},{4,5},{5,6},{6,7},{7,8},{8,9},{9,10},{10,1... | collective-permute-start | bytes 2359304 | tf_op jit(solution)/shard_map/ppermute | solution.py:27
  267.0 8.7 %copy-start.10 = (bf16[8192,256]{1,0:T(8,128)(2,1)S(1)}, bf16[8192,256]{1,0:T(8,128)(2,1)}, u32[]{:S(2)}) copy-start(bf16[8192,256]{1,0:T(8,128)(2,1)} %param.6) | copy-start | bytes 12582916
Sparse Core Ops, SparseCore 0:
  10.5 64.1 all-gather.4
  77.8 63.4 all-gather.2
